TPU v7x, 512 devices: a whole 4x8x8 slice. The times are simulated.
512 devices in a mesh: tm: 32 (over x, y), user: 16 (over z, core).
Axes of the slice: x: 4, y: 8, z: 8, core: 2. Of those that a mesh axis runs over, the one named last changes fastest.
Arguments:
- events: bfloat16 [16, 32768, 512], P('user', 'tm'), may hold values from -6 to 6
- w_first: bfloat16 [512, 1024], replicated, may hold values from -0.25 to 0.25
- b_first: float32 [1024], replicated, may hold values from -3 to 3
- w_second: bfloat16 [1024, 512], replicated, may hold values from -0.1875 to 0.1875
- count_embed: float32 [512], replicated, may hold values from -0.3 to 0.3
- norm_gain: float32 [512], replicated, may hold values from 0.5 to 1.5
- event_session: int32 [16, 32768], P('user', 'tm'), may hold values from 0 to 2047, as said below
- event_count: int32 [16, 32], P('user', 'tm'), may hold values from 256 to 1024, as said below
- session_user: int32 [16, 2048], P('user', 'tm'), may hold values from 0 to 65535, as said below
Outputs:
- section_rows: bfloat16 [32, 16, 128, 512], P('tm', 'user')
- section_users: int32 [32, 16, 128], P('tm', 'user')
Inputs may be any that keep to these rules, and one draw needn't show every extreme that they name: `event_session`: the events of time slice t (slots t * 1024 to (t + 1) * 1024 - 1 of a shard) name sessions of slices max(0, t - 16) to t only; some sessions have no valid event. `event_count`: some time slice of some shard has all 1024 events valid. `session_user`: among the 64 sessions of one shard and time slice, at most 8 have users of the same section (user mod 16); in every time slice some section gets exactly 8 from every shard.
All inputs are finite; a program needn't handle non-finite values.
Results may differ from a plain program's by a relative error of at most 0.0042.
Values may be sent and summed in bfloat16 or wider, within the bound.
No kernel may reach another device: no remote copies, remote signals or barrier semaphores. Data moves between devices by JAX's collectives and lax.ppermute only.
A program may use at most 64 MiB of HBM per device.

v0:
```python
import jax
import jax.numpy as jnp
from jax import lax
from jax.sharding import PartitionSpec as P


def on_device(
    events,
    w_first,
    b_first,
    w_second,
    count_embed,
    norm_gain,
    event_session,
    event_count,
    session_user,
):
    event_rows = events[0]
    ev_rows = event_rows.shape[0]
    width = event_rows.shape[1]
    sess_dev = session_user.shape[1]
    n_tm = lax.axis_size("tm")
    n_sec = lax.axis_size("user")
    capacity = max(2, 2 * sess_dev // n_sec)
    valid_count = event_count[0, 0]
    hidden = jax.nn.gelu(
        jnp.dot(event_rows, w_first, preferred_element_type=jnp.float32) + b_first
    ).astype(jnp.bfloat16)
    vectors = jnp.dot(hidden, w_second, preferred_element_type=jnp.float32).astype(jnp.bfloat16)
    valid = jnp.arange(ev_rows, dtype=jnp.int32) < valid_count
    session_ids = event_session[0]
    local_ids = jnp.arange(sess_dev, dtype=jnp.int32)
    assign = (
        session_ids[None, :] == jnp.arange(n_tm * sess_dev, dtype=jnp.int32)[:, None]
    ) & valid[None, :]
    partial_value = jnp.dot(
        assign.astype(jnp.bfloat16), vectors, preferred_element_type=jnp.float32
    )
    totals = jnp.sum(assign.astype(jnp.float32), axis=1)
    partial_value, counted = (partial_value, totals)
    sums, totals = (
        lax.psum_scatter(partial_value, "tm", scatter_dimension=0, tiled=True),
        lax.psum_scatter(counted, "tm", scatter_dimension=0, tiled=True),
    )
    averaged = sums / jnp.maximum(totals, 1.0)[:, None]
    mixed = averaged + jnp.log1p(totals)[:, None] * count_embed
    scaled = mixed * lax.rsqrt(jnp.mean(mixed * mixed, axis=-1, keepdims=True) + 1e-06) * norm_gain
    session_rows = scaled.astype(jnp.bfloat16)
    users = session_user[0]
    section = users % n_sec
    same = section[:, None] == section[None, :]
    before = local_ids[:, None] > local_ids[None, :]
    rank = jnp.sum((same & before).astype(jnp.int32), axis=1)
    slot = section * capacity + rank
    assign_slot = slot[None, :] == jnp.arange(n_sec * capacity, dtype=jnp.int32)[:, None]
    outgoing = jnp.dot(
        assign_slot.astype(jnp.bfloat16), session_rows, preferred_element_type=jnp.float32
    )
    outgoing = outgoing.astype(jnp.bfloat16).reshape(n_sec, capacity, width)
    outgoing_users = jnp.sum(jnp.where(assign_slot, users[None, :] + 1, 0), axis=1) - 1
    outgoing_users = outgoing_users.reshape(n_sec, capacity)
    arrived, arrived_users = (
        lax.all_to_all(outgoing, "user", split_axis=0, concat_axis=0, tiled=True),
        lax.all_to_all(outgoing_users, "user", split_axis=0, concat_axis=0, tiled=True),
    )
    section_rows = arrived.reshape(1, 1, n_sec * capacity, width)
    section_users = arrived_users.reshape(1, 1, n_sec * capacity)
    return (section_rows, section_users)


def solution(mesh):
    in_specs = (
        P("user", "tm", None),
        P(),
        P(),
        P(),
        P(),
        P(),
        P("user", "tm"),
        P("user", "tm"),
        P("user", "tm"),
    )
    out_specs = (P("tm", "user", None, None), P("tm", "user", None))
    return jax.shard_map(
        on_device, mesh=mesh, in_specs=in_specs, out_specs=out_specs, check_vma=False
    )
```

profile of v0, /device:TPU:1, one launch (start us, length us, event | category | flops | bytes accessed | tf_op | source)
XLA Modules:
  0.0 278.3 jit_solution(7379250407643766242)
XLA Ops:
  7.2 0.0 copy-start
  7.2 0.0 reduce-scatter.2.cloned.1.call-start
  8.0 0.4 copy-done
  8.4 0.0 copy-start.2
  8.4 4.1 %convolution_convert_fusion = bf16[1024,512]{1,0:T(8,128)(2,1)S(1)} fusion(bf16[1024,512]{1,0:T(8,128)(2,1)S(1)} %copy-done, bf16[512,1024]{1,0:T(8,128)(2,1)} %param.10, f32[1024]{0:T(1024)} %param.11, bf16[1,1024,512]{2,1,0:T(8,128)(2,1)} %param.9), kind=kOutput, calls=%fused_computation.15 | convolution fusion | flops 2158493696 | bytes 4198400 | tf_op jit(solution)/shard_map/dot_general | solution.py:29
  12.5 0.0 copy-done.2
  12.5 4.3 %fusion.1 = f32[2048,512]{1,0:T(8,128)} fusion(bf16[1024,512]{1,0:T(8,128)(2,1)S(1)} %convolution_convert_fusion, s32[1024]{0:T(1024)S(1)} %bitcast.28, pred[1024]{0:T(1024)(128)(4,1)S(1)} %iota_compare_fusion.4), kind=kOutput, calls=%fused_computation.3 | convolution fusion | flops 2151677952 | bytes 5248000 | tf_op jit(solution)/shard_map/dot_general | solution.py:36
  16.8 0.0 copy-start.4
  16.8 0.0 copy-start.1
  16.8 0.0 copy-start.3
  16.8 0.0 reduce-scatter.2.cloned.1.call-update
  16.8 0.6 copy-done.4
  17.4 0.2 convert_reduce_fusion.1
  17.6 0.1 select_reduce_fusion
  17.7 0.7 sub.7
  18.4 11.8 %all-to-all-start.1 = ((s32[16,1,8]{2,1,0:T(1,128)}), s32[16,1,8]{2,1,0:T(1,128)S(1)}, u32[]{:S(2)}, u32[]{:S(2)}) async-start(s32[16,1,8]{2,1,0:T(1,128)} %bitcast.10), calls=%async_computation.2 | async-start | bytes 16384 | tf_op jit(solution)/shard_map/all_to_all | solution.py:64
  30.2 1.3 dynamic-slice
  32.2 1.5 convert_reduce_fusion
  33.6 62.7 %all-reduce = f32[2048]{0:T(1024)S(1)} all-reduce(f32[2048]{0:T(1024)S(1)} %convert_reduce_fusion), channel_id=3, replica_groups=mesh['tm'=32,'user'=16] {'tm'}, use_global_device_ids=true, to_apply=%region_3.0.clone | all-reduce | flops 2048 | bytes 16384
  96.3 0.1 broadcast_maximum_fusion
  96.4 150.1 %reduce-scatter.2.cloned.1.call-done = f32[64,512]{1,0:T(8,128)} async-done(((f32[2048,512]{1,0:T(8,128)}), f32[64,512]{1,0:T(8,128)}) %reduce-scatter.2.cloned.1.call-update) | async-done | bytes 131088 | tf_op jit(solution)/shard_map/reduce_scatter | solution.py:42
  246.5 0.0 copy-done.1
  246.5 1.1 multiply_reduce_fusion
  247.6 0.0 copy-done.3
  247.6 1.9 fusion.13
  249.4 0.0 all-to-all-done.1
  249.4 12.5 %all-to-all-start = ((bf16[16,8,512]{2,1,0:T(8,128)(2,1)}), bf16[16,8,512]{2,1,0:T(8,128)(2,1)S(1)}, u32[]{:S(2)}, u32[]{:S(2)}) async-start(bf16[16,8,512]{2,1,0:T(8,128)(2,1)} %fusion.13), calls=%async_computation.1 | async-start | bytes 262144 | tf_op jit(solution)/shard_map/all_to_all | solution.py:63
  262.0 0.5 broadcast.80
  262.5 0.7 reduce.3
  263.1 0.6 reshape.71
  263.7 7.1 %all-to-all-done = bf16[16,8,512]{2,1,0:T(8,128)(2,1)S(1)} async-done(((bf16[16,8,512]{2,1,0:T(8,128)(2,1)}), bf16[16,8,512]{2,1,0:T(8,128)(2,1)S(1)}, u32[]{:S(2)}, u32[]{:S(2)}) %all-to-all-start) | async-done | bytes 131104 | tf_op jit(solution)/shard_map/all_to_all | solution.py:63
  270.8 0.7 copy.15
  (6 shorter events, 0.0 us)
Async XLA Ops:
  7.2 1.2 copy-start
  7.2 239.3 %reduce-scatter.2.cloned.1.call-start = ((), (), s32[]{:S(2)}) async-start(), calls=%async_computation.3 | async-start | bytes 4325376 | tf_op jit(solution)/shard_map/reduce_scatter | solution.py:42
  8.4 4.1 %copy-start.2 = (s32[1,1024]{1,0:T(1,128)S(1)}, s32[1,1024]{1,0:T(1,128)}, u32[]{:S(2)}) copy-start(s32[1,1024]{1,0:T(1,128)} %param.15) | copy-start | bytes 12292
  16.8 0.7 copy-start.4
  16.8 229.7 %copy-start.1 = (f32[512]{0:T(512)S(1)}, f32[512]{0:T(512)}, u32[]{:S(2)}) copy-start(f32[512]{0:T(512)} %param.13) | copy-start | bytes 6148
  16.8 230.8 %copy-start.3 = (f32[512]{0:T(512)S(1)}, f32[512]{0:T(512)}, u32[]{:S(2)}) copy-start(f32[512]{0:T(512)} %param.14) | copy-start | bytes 6148
  18.4 231.0 %all-to-all-start.1 = ((s32[16,1,8]{2,1,0:T(1,128)}), s32[16,1,8]{2,1,0:T(1,128)S(1)}, u32[]{:S(2)}, u32[]{:S(2)}) async-start(s32[16,1,8]{2,1,0:T(1,128)} %bitcast.10), calls=%async_computation.2 | async-start | bytes 16384 | tf_op jit(solution)/shard_map/all_to_all | solution.py:64
  249.4 21.4 %all-to-all-start = ((bf16[16,8,512]{2,1,0:T(8,128)(2,1)}), bf16[16,8,512]{2,1,0:T(8,128)(2,1)S(1)}, u32[]{:S(2)}, u32[]{:S(2)}) async-start(bf16[16,8,512]{2,1,0:T(8,128)(2,1)} %fusion.13), calls=%async_computation.1 | async-start | bytes 262144 | tf_op jit(solution)/shard_map/all_to_all | solution.py:63
Sparse Core Ops, SparseCore 0:
  16.9 229.4 reduce-scatter.1
where the time goes:
time: 279 us; the launch traced here: 278 us
  waiting for transfers between devices  157 us (56%)
  blocking collectives  62.7 us (22%)
  starting transfers between devices  24.4 us (9%)
  between operations  15.5 us (6%)
  matrix products  10.2 us (4%)
  local copies, waits for them, and re-layouts  4.81 us (2%)
  other arithmetic  3.64 us (1%)
    reduce_scatter x1, waiting for transfers between devices, on_device(): lax.psum_scatter(partial_value, 'tm', scatter_dimension=0, tiled=True)  150 us
    unnamed x1, blocking collectives  62.7 us
    all_to_all x1, starting transfers between devices, on_device(): lax.all_to_all(outgoing, 'user', split_axis=0, concat_axis=0, tiled=True)  12.5 us
    all_to_all x1, starting transfers between devices, on_device(): lax.all_to_all(outgoing_users, 'user', split_axis=0, concat_axis=0, tiled...  11.8 us
    all_to_all x1, waiting for transfers between devices, on_device(): lax.all_to_all(outgoing, 'user', split_axis=0, concat_axis=0, tiled=True)  7.1 us
  transfers between devices with their start and end apart: 3, of which 2 were waited for; matrix products, arithmetic and copies ran while one was open for 3% of the time, Pallas kernels for 0%

commit v1 on v0

v1 whole, which is shorter than its diff:
```python
import functools

import jax
import jax.numpy as jnp
from jax import lax
from jax.experimental import pallas as pl
from jax.experimental.pallas import tpu as pltpu
from jax.sharding import PartitionSpec as P

LANES = 128
DIGIT = 256.0


def count_tile(row):
    high = jnp.floor(row * (1.0 / DIGIT))
    low = row - high * DIGIT
    at = lax.broadcasted_iota(jnp.int32, (8, LANES), 0)
    return jnp.where(at == 0, high, jnp.where(at == 1, low, 0.0))


def embed_kernel(window, sess, count_ref, ev_ref, w1_ref, b1_ref, w2_ref, ids_ref, out_ref, far_ref, vec, acc):
    rows, width = ev_ref.shape
    groups = width // LANES
    pick = window * sess
    t = lax.axis_index("tm")
    step = 256
    for c in range(rows // step):
        at = pl.ds(c * step, step)
        h = jnp.dot(ev_ref[at, :], w1_ref[...], preferred_element_type=jnp.float32)
        h = jax.nn.gelu(h + b1_ref[...]).astype(jnp.bfloat16)
        vec[at, :width] = jnp.dot(h, w2_ref[...], preferred_element_type=jnp.float32).astype(jnp.bfloat16)
        vec[at, width:] = jnp.ones((step, LANES), jnp.bfloat16)
    ids = ids_ref[...]
    far = (ids // sess) == t - window
    target = jnp.where(far, pick + ids % LANES, ids % pick)
    valid = lax.broadcasted_iota(jnp.int32, ids.shape, 1) < count_ref[0, 0]
    target = jnp.where(valid, target, -1)
    total = pick + LANES
    onehot = lax.broadcasted_iota(jnp.int32, (total, rows), 0) == target
    acc[...] = jnp.dot(
        jnp.where(onehot, 1.0, 0.0).astype(jnp.bfloat16), vec[...], preferred_element_type=jnp.float32
    )
    eye = lax.broadcasted_iota(jnp.int32, (LANES, LANES), 0) == lax.broadcasted_iota(
        jnp.int32, (LANES, LANES), 1
    )
    per = LANES // sess
    for c in range(total // LANES):
        counted = acc[c * LANES : (c + 1) * LANES, width:]
        tile = count_tile(jnp.sum(jnp.where(eye, counted, 0.0), axis=0, keepdims=True)).astype(jnp.bfloat16)
        if c < pick // LANES:
            for b in range(per):
                r = c * per + b
                for g in range(groups):
                    out_ref[r, g * sess : (g + 1) * sess, :] = acc[
                        r * sess : (r + 1) * sess, g * LANES : (g + 1) * LANES
                    ].astype(jnp.bfloat16)
                out_ref[r, groups * sess :, :] = tile
        else:
            start = pl.multiple_of(pick + sess * lax.rem(t, per), sess)
            for g in range(groups):
                far_ref[g * sess : (g + 1) * sess, :] = acc[
                    pl.ds(start, sess), g * LANES : (g + 1) * LANES
                ].astype(jnp.bfloat16)
            far_ref[groups * sess :, :] = tile


def far_kernel(window, recv_ref, far_ref, out_ref):
    me = lax.rem(lax.axis_index("tm"), window)
    total = far_ref[...].astype(jnp.float32)
    for j in range(window - 1):
        total += jnp.where(j < me, recv_ref[j].astype(jnp.float32), 0.0)
    data = total.shape[0] - 8
    out_ref[:data, :] = total[:data].astype(jnp.bfloat16)
    out_ref[data:, :] = count_tile(DIGIT * total[data : data + 1] + total[data + 1 : data + 2]).astype(jnp.bfloat16)


def near_kernel(window, recv_ref, out_ref):
    me = lax.rem(lax.axis_index("tm"), window)
    total = recv_ref[window - 1].astype(jnp.float32)
    for j in range(window - 1):
        total += jnp.where(j >= me, recv_ref[j].astype(jnp.float32), 0.0)
    out_ref[...] = total


def pack_kernel(n_sec, near_ref, got_ref, embed_ref, gain_ref, users_ref, out_ref):
    sess = users_ref.shape[1]
    width = embed_ref.shape[1]
    groups = width // LANES
    slots = out_ref.shape[0]
    capacity = slots // n_sec
    t = lax.axis_index("tm")
    total = near_ref[...] + got_ref[...].astype(jnp.float32)
    data = groups * sess
    counts = DIGIT * total[data : data + 1] + total[data + 1 : data + 2]
    spot = lax.broadcasted_iota(jnp.int32, (sess, LANES), 0) + sess * lax.rem(t, LANES // sess)
    mine = spot == lax.broadcasted_iota(jnp.int32, (sess, LANES), 1)
    counts = jnp.sum(jnp.where(mine, counts, 0.0), axis=1, keepdims=True)
    least = jnp.maximum(counts, 1.0)
    weight = jnp.log1p(counts)
    mixed = [
        total[g * sess : (g + 1) * sess] / least + weight * embed_ref[:, g * LANES : (g + 1) * LANES]
        for g in range(groups)
    ]
    square = sum(m * m for m in mixed)
    scale = lax.rsqrt(jnp.sum(square, axis=1, keepdims=True) / width + 1e-06)
    session_rows = jnp.concatenate(
        [(m * scale * gain_ref[:, g * LANES : (g + 1) * LANES]).astype(jnp.bfloat16) for g, m in enumerate(mixed)],
        axis=1,
    )
    users = users_ref[...]
    section = lax.rem(users, n_sec)
    i0 = lax.broadcasted_iota(jnp.int32, (sess, sess), 0)
    i1 = lax.broadcasted_iota(jnp.int32, (sess, sess), 1)
    section_column = jnp.sum(jnp.where(i0 == i1, section, 0), axis=1, keepdims=True)
    rank = jnp.sum(jnp.where((section_column == section) & (i0 < i1), 1, 0), axis=0, keepdims=True)
    slot = section * capacity + rank
    assign = lax.broadcasted_iota(jnp.int32, (slots, sess), 0) == slot
    placed = jnp.dot(
        jnp.where(assign, 1.0, 0.0).astype(jnp.bfloat16), session_rows, preferred_element_type=jnp.float32
    )
    out_ref[:, :width] = placed.astype(jnp.bfloat16)
    named = jnp.sum(jnp.where(assign, (users + 1).astype(jnp.float32), 0.0), axis=1, keepdims=True)
    high = jnp.floor(named * (1.0 / DIGIT))
    low = named - high * DIGIT
    lane = lax.broadcasted_iota(jnp.int32, (slots, LANES), 1)
    out_ref[:, width:] = jnp.where(lane == 0, high, jnp.where(lane == 1, low, 0.0)).astype(jnp.bfloat16)


def unpack_kernel(got_ref, rows_ref, users_ref):
    slots = got_ref.shape[0]
    width = rows_ref.shape[1]
    rows_ref[...] = got_ref[:, :width]
    digits = got_ref[:, width:].astype(jnp.float32)
    lane = lax.broadcasted_iota(jnp.int32, digits.shape, 1)
    column = jnp.sum(jnp.where(lane == 0, DIGIT * digits, jnp.where(lane == 1, digits, 0.0)), axis=1, keepdims=True)
    eye = lax.broadcasted_iota(jnp.int32, (slots, slots), 0) == lax.broadcasted_iota(jnp.int32, (slots, slots), 1)
    users_ref[...] = jnp.sum(jnp.where(eye, column, 0.0), axis=0, keepdims=True).astype(jnp.int32) - 1


def on_device(
    events,
    w_first,
    b_first,
    w_second,
    count_embed,
    norm_gain,
    event_session,
    event_count,
    session_user,
):
    rows, width = events.shape[1:]
    sess = session_user.shape[1]
    n_tm = lax.axis_size("tm")
    n_sec = lax.axis_size("user")
    capacity = max(2, 2 * sess // n_sec)
    window = n_tm // 2
    block = width // LANES * sess + 8
    bf16, f32 = jnp.bfloat16, jnp.float32
    vmem = pl.BlockSpec(memory_space=pltpu.VMEM)
    smem = pl.BlockSpec(memory_space=pltpu.SMEM)
    shape = jax.ShapeDtypeStruct
    blocks, far = pl.pallas_call(
        functools.partial(embed_kernel, window, sess),
        out_shape=(shape((window, block, LANES), bf16), shape((block, LANES), bf16)),
        in_specs=[smem] + [vmem] * 5,
        out_specs=(vmem, vmem),
        scratch_shapes=[
            pltpu.VMEM((rows, width + LANES), bf16),
            pltpu.VMEM((window * sess + LANES, width + LANES), f32),
        ],
        name="embed",
    )(event_count, events[0], w_first, b_first[None], w_second, event_session)
    groups = [[first + j for j in range(window)] for first in range(0, n_tm, window)]
    arrived = lax.all_to_all(blocks, "tm", 0, 0, tiled=True, axis_index_groups=groups)
    far = pl.pallas_call(
        functools.partial(far_kernel, window),
        out_shape=shape((block, LANES), bf16),
        in_specs=[vmem, vmem],
        out_specs=vmem,
        name="far",
    )(arrived, far)
    got = lax.ppermute(far, "tm", [(t, t - window) for t in range(window, n_tm)])
    near = pl.pallas_call(
        functools.partial(near_kernel, window),
        out_shape=shape((block, LANES), f32),
        in_specs=[vmem],
        out_specs=vmem,
        name="near",
    )(arrived)
    outgoing = pl.pallas_call(
        functools.partial(pack_kernel, n_sec),
        out_shape=shape((n_sec * capacity, width + LANES), bf16),
        in_specs=[vmem] * 5,
        out_specs=vmem,
        name="pack",
    )(near, got, count_embed[None], norm_gain[None], session_user)
    routed = lax.all_to_all(
        outgoing.reshape(n_sec, capacity, width + LANES), "user", 0, 0, tiled=True
    ).reshape(n_sec * capacity, width + LANES)
    section_rows, section_users = pl.pallas_call(
        unpack_kernel,
        out_shape=(shape((n_sec * capacity, width), bf16), shape((1, n_sec * capacity), jnp.int32)),
        in_specs=[vmem],
        out_specs=(vmem, vmem),
        name="unpack",
    )(routed)
    return (section_rows[None, None], section_users[None])


def solution(mesh):
    in_specs = (
        P("user", "tm", None),
        P(),
        P(),
        P(),
        P(),
        P(),
        P("user", "tm"),
        P("user", "tm"),
        P("user", "tm"),
    )
    out_specs = (P("tm", "user", None, None), P("tm", "user", None))
    return jax.shard_map(
        on_device, mesh=mesh, in_specs=in_specs, out_specs=out_specs, check_vma=False
    )
```

time: 279 us -> 83 us (0.30)
  waiting for transfers between devices: 157 us -> 4.12 us
  starting transfers between devices: 24.4 us -> 1.28 us
  Pallas kernels: 0 us -> 15.3 us
  between operations: 15.5 us -> 1.29 us
  matrix products: 10.2 us -> 0 us
  local copies, waits for them, and re-layouts: 4.81 us -> 0.63 us
  other arithmetic: 3.64 us -> 0 us
    reduce_scatter x1 -> x0, waiting for transfers between devices: 150 us -> none  [on_device(): lax.psum_scatter(partial_value, 'tm', scatter_dimension=0, tiled=True)]
    unnamed x1 -> x0, blocking collectives: 62.7 us -> none
    all_to_all x0 -> x2, blocking collectives: none -> 60 us  [the longest x1 35.3 us: on_device(): lax.all_to_all(blocks, 'tm', 0, 0, tiled=True, axis_index_groups=groups)]
    all_to_all x2 -> x0, starting transfers between devices: 24.3 us -> none  [the longest x1 12.5 us: on_device(): lax.all_to_all(outgoing, 'user', split_axis=0, concat_axis=0, tiled=True)]
    pallas_call x0 -> x5, Pallas kernels: none -> 15.3 us  [the longest x1 7.54 us: on_device(): pl.pallas_call(functools.partial(embed_kernel, window, sess), out_shape=(...]
    dot_general x3 -> x0, matrix products: 10.2 us -> none  [the longest x1 4.28 us: on_device(): jnp.dot(assign.astype(jnp.bfloat16), vectors, preferred_element_type=jnp....]
    all_to_all x2 -> x0, waiting for transfers between devices: 7.1 us -> none  [the longest x1 7.1 us: on_device(): lax.all_to_all(outgoing, 'user', split_axis=0, concat_axis=0, tiled=True)]
    ppermute x0 -> x1, waiting for transfers between devices: none -> 4.12 us  [on_device(): lax.ppermute(far, 'tm', [(t, t - window) for t in range(window, n_tm)])]
  transfers between devices with their start and end apart: 3 -> 1, of which waited for: 2 -> 1; matrix products, arithmetic and copies ran while one was open for 3% -> 0% of each run, Pallas kernels for 0% -> 3%
where the time goes in v1:
time: 83 us; the launch traced here: 82.6 us
  blocking collectives  60 us (72%)
  Pallas kernels  15.3 us (18%)
  waiting for transfers between devices  4.12 us (5%)
  between operations  1.29 us (2%)
  starting transfers between devices  1.28 us (2%)
    all_to_all x1, blocking collectives, on_device(): lax.all_to_all(blocks, 'tm', 0, 0, tiled=True, axis_index_groups=groups)  35.3 us
    all_to_all x1, blocking collectives, on_device(): lax.all_to_all(outgoing.reshape(n_sec, capacity, width + LANES), 'user',...  24.7 us
    pallas_call x1, Pallas kernels, on_device(): pl.pallas_call(functools.partial(embed_kernel, window, sess), out_shape=(...  7.54 us
    ppermute x1, waiting for transfers between devices, on_device(): lax.ppermute(far, 'tm', [(t, t - window) for t in range(window, n_tm)])  4.12 us
    pallas_call x1, Pallas kernels, on_device(): pl.pallas_call(functools.partial(near_kernel, window), out_shape=shape((b...  2.11 us
    pallas_call x1, Pallas kernels, on_device(): pl.pallas_call(functools.partial(far_kernel, window), out_shape=shape((bl...  2.08 us
    pallas_call x1, Pallas kernels, on_device(): pl.pallas_call(functools.partial(pack_kernel, n_sec), out_shape=shape((n_...  1.98 us
  transfers between devices with their start and end apart: 1, of which 1 were waited for; matrix products, arithmetic and copies ran while one was open for 0% of the time, Pallas kernels for 3%

profile of v1, /device:TPU:1, one launch (start us, length us, event | category | flops | bytes accessed | tf_op | source)
XLA Modules:
  0.0 82.6 jit_solution(13086156915225389071)
XLA Ops:
  1.3 7.5 %embed.1 = (bf16[16,264,128]{2,1,0:T(8,128)(2,1)}, bf16[264,128]{1,0:T(8,128)(2,1)}) custom-call(s32[1,1]{1,0:T(1,128)S(6)} %copy.11.count_ref, bf16[1024,512]{1,0:T(8,128)(2,1)} %bitcast.8, bf16[512,1024]{1,0:T(8,128)(2,1)} %w1_ref.1, f32[1,1024]{1,0:T(1,128)} %bitcast.11, bf16[1024,512]{1,0:T(8,128)(2,1)} %w2_ref.1, s32[1,1024]{1,0:T(1,128)} %ids_ref.1), custom_call_target="tpu_custom_call" | custom-call | tf_op jit(solution)/shard_map/embed/pallas_call | solution.py:162
  8.8 35.3 %all_to_all.10.recv_ref = bf16[16,264,128]{2,1,0:T(8,128)(2,1)} all-to-all(bf16[16,264,128]{2,1,0:T(8,128)(2,1)} %get-tuple-element.6), channel_id=1, replica_groups={{0,16,32,48,64,80,96,112,128,144,160,176,192,208,224,240},{256,272,288,..., dimensions={0} | all-to-all | bytes 2162688 | tf_op jit(solution)/shard_map/all_to_all | solution.py:174
  44.1 2.1 %far.1 = bf16[264,128]{1,0:T(8,128)(2,1)} custom-call(bf16[16,264,128]{2,1,0:T(8,128)(2,1)} %all_to_all.10.recv_ref, bf16[264,128]{1,0:T(8,128)(2,1)} %get-tuple-element.7.far_ref), custom_call_target="tpu_custom_call" | custom-call | tf_op jit(solution)/shard_map/far/pallas_call | solution.py:175
  46.2 1.3 %collective-permute-start = (bf16[264,128]{1,0:T(8,128)(2,1)}, bf16[264,128]{1,0:T(8,128)(2,1)S(1)}, u32[]{:S(2)}, u32[]{:S(2)}) collective-permute-start(bf16[264,128]{1,0:T(8,128)(2,1)} %far.1), channel_id=1, source_target_pairs={{256,0},{272,16},{288,32},{304,48},{320,64},{336,80},{352,96},{368... | collective-permute-start | bytes 202760 | tf_op jit(solution)/shard_map/ppermute | solution.py:182
  47.5 2.1 %near.1.near_ref = f32[264,128]{1,0:T(8,128)} custom-call(bf16[16,264,128]{2,1,0:T(8,128)(2,1)} %all_to_all.10.recv_ref), custom_call_target="tpu_custom_call" | custom-call | tf_op jit(solution)/shard_map/near/pallas_call | solution.py:183
  49.6 4.1 %collective-permute-done.got_ref = bf16[264,128]{1,0:T(8,128)(2,1)S(1)} collective-permute-done((bf16[264,128]{1,0:T(8,128)(2,1)}, bf16[264,128]{1,0:T(8,128)(2,1)S(1)}, u32[]{:S(2)}, u32[]{:S(2)}) %collective-permute-start) | collective-permute-done | bytes 67616 | tf_op jit(solution)/shard_map/ppermute | solution.py:182
  53.7 0.0 copy-start
  53.7 0.6 copy-done
  54.3 2.0 %pack.1 = bf16[128,640]{1,0:T(8,128)(2,1)} custom-call(f32[264,128]{1,0:T(8,128)} %near.1.near_ref, bf16[264,128]{1,0:T(8,128)(2,1)} %copy-done, f32[1,512]{1,0:T(1,128)} %bitcast.12, f32[1,512]{1,0:T(1,128)} %bitcast.13, s32[1,64]{1,0:T(1,128)} %users_ref.1), custom_call_target="tpu_custom_call" | custom-call | tf_op jit(solution)/shard_map/pack/pallas_call | solution.py:190
  56.3 24.7 %all_to_all.11 = bf16[16,8,640]{2,1,0:T(8,128)(2,1)} all-to-all(bf16[16,8,640]{2,1,0:T(8,128)(2,1)} %bitcast.10), channel_id=1, replica_groups=mesh['tm'=32,'user'=16] {'user'}, dimensions={0} | all-to-all | bytes 327680 | tf_op jit(solution)/shard_map/all_to_all | solution.py:197
  81.0 1.6 %unpack.1 = (bf16[128,512]{1,0:T(8,128)(2,1)}, s32[1,128]{1,0:T(1,128)}) custom-call(bf16[128,640]{1,0:T(8,128)(2,1)} %bitcast.9), custom_call_target="tpu_custom_call" | custom-call | tf_op jit(solution)/shard_map/unpack/pallas_call | solution.py:200
Async XLA Ops:
  46.2 7.5 %collective-permute-start = (bf16[264,128]{1,0:T(8,128)(2,1)}, bf16[264,128]{1,0:T(8,128)(2,1)S(1)}, u32[]{:S(2)}, u32[]{:S(2)}) collective-permute-start(bf16[264,128]{1,0:T(8,128)(2,1)} %far.1), channel_id=1, source_target_pairs={{256,0},{272,16},{288,32},{304,48},{320,64},{336,80},{352,96},{368... | collective-permute-start | bytes 202760 | tf_op jit(solution)/shard_map/ppermute | solution.py:182
  53.7 0.6 copy-start

commit v2 on v1

--- a/solution.py
+++ b/solution.py
@@ -33,7 +33,7 @@
     ids = ids_ref[...]
     far = (ids // sess) == t - window
     target = jnp.where(far, pick + ids % LANES, ids % pick)
-    valid = lax.broadcasted_iota(jnp.int32, ids.shape, 1) < count_ref[0, 0]
+    valid = lax.broadcasted_iota(jnp.int32, ids.shape, 1) < count_ref[...]
     target = jnp.where(valid, target, -1)
     total = pick + LANES
     onehot = lax.broadcasted_iota(jnp.int32, (total, rows), 0) == target
@@ -157,12 +157,13 @@
     block = width // LANES * sess + 8
     bf16, f32 = jnp.bfloat16, jnp.float32
     vmem = pl.BlockSpec(memory_space=pltpu.VMEM)
-    smem = pl.BlockSpec(memory_space=pltpu.SMEM)
     shape = jax.ShapeDtypeStruct
+    kept = pltpu.VMEM
+    pin = functools.partial(pltpu.with_memory_space_constraint, memory_space=pltpu.VMEM)
     blocks, far = pl.pallas_call(
         functools.partial(embed_kernel, window, sess),
-        out_shape=(shape((window, block, LANES), bf16), shape((block, LANES), bf16)),
-        in_specs=[smem] + [vmem] * 5,
+        out_shape=(kept((window, block, LANES), bf16), kept((block, LANES), bf16)),
+        in_specs=[vmem] * 6,
         out_specs=(vmem, vmem),
         scratch_shapes=[
             pltpu.VMEM((rows, width + LANES), bf16),
@@ -174,26 +175,26 @@
     arrived = lax.all_to_all(blocks, "tm", 0, 0, tiled=True, axis_index_groups=groups)
     far = pl.pallas_call(
         functools.partial(far_kernel, window),
-        out_shape=shape((block, LANES), bf16),
+        out_shape=kept((block, LANES), bf16),
         in_specs=[vmem, vmem],
         out_specs=vmem,
         name="far",
-    )(arrived, far)
+    )(pin(arrived), pin(far))
     got = lax.ppermute(far, "tm", [(t, t - window) for t in range(window, n_tm)])
     near = pl.pallas_call(
         functools.partial(near_kernel, window),
-        out_shape=shape((block, LANES), f32),
+        out_shape=kept((block, LANES), f32),
         in_specs=[vmem],
         out_specs=vmem,
         name="near",
-    )(arrived)
+    )(pin(arrived))
     outgoing = pl.pallas_call(
         functools.partial(pack_kernel, n_sec),
-        out_shape=shape((n_sec * capacity, width + LANES), bf16),
+        out_shape=kept((n_sec * capacity, width + LANES), bf16),
         in_specs=[vmem] * 5,
         out_specs=vmem,
         name="pack",
-    )(near, got, count_embed[None], norm_gain[None], session_user)
+    )(pin(near), pin(got), count_embed[None], norm_gain[None], session_user)
     routed = lax.all_to_all(
         outgoing.reshape(n_sec, capacity, width + LANES), "user", 0, 0, tiled=True
     ).reshape(n_sec * capacity, width + LANES)
@@ -203,7 +204,7 @@
         in_specs=[vmem],
         out_specs=(vmem, vmem),
         name="unpack",
-    )(routed)
+    )(pin(routed))
     return (section_rows[None, None], section_users[None])
 
 

time: 83 us -> 76.8 us (0.925)
  Pallas kernels: 15.3 us -> 8.74 us
  waiting for transfers between devices: 4.12 us -> 5.01 us
    pallas_call x3, Pallas kernels: 6.17 us -> 1.53 us  [the longest x1 1.07 us: on_device(): pl.pallas_call(functools.partial(pack_kernel, n_sec), out_shape=kept((n_s...]
    all_to_all x1, blocking collectives: 35.3 us -> 36.9 us  [on_device(): lax.all_to_all(blocks, 'tm', 0, 0, tiled=True, axis_index_groups=groups)]
    all_to_all x1, blocking collectives: 24.7 us -> 23.3 us  [on_device(): lax.all_to_all(outgoing.reshape(n_sec, capacity, width + LANES), 'user',...]
    pallas_call x1, Pallas kernels: 7.54 us -> 6.54 us  [on_device(): pl.pallas_call(functools.partial(embed_kernel, window, sess), out_shape=(...]
    pallas_call x1, Pallas kernels: 1.59 us -> 0.67 us  [on_device(): pl.pallas_call(unpack_kernel, out_shape=(shape((n_sec * capacity, width),...]
    ppermute x1, waiting for transfers between devices: 4.12 us -> 5.01 us  [on_device(): lax.ppermute(far, 'tm', [(t, t - window) for t in range(window, n_tm)])]
  transfers between devices with their start and end apart: 1 -> 1, of which waited for: 1 -> 1; matrix products, arithmetic and copies ran while one was open for 0% -> 0% of each run, Pallas kernels for 3% -> 0%
where the time goes in v2:
time: 76.8 us; the launch traced here: 76.5 us
  blocking collectives  60.2 us (78%)
  Pallas kernels  8.74 us (11%)
  waiting for transfers between devices  5.01 us (7%)
  between operations  1.31 us (2%)
  starting transfers between devices  1.29 us (2%)
    all_to_all x1, blocking collectives, on_device(): lax.all_to_all(blocks, 'tm', 0, 0, tiled=True, axis_index_groups=groups)  36.9 us
    all_to_all x1, blocking collectives, on_device(): lax.all_to_all(outgoing.reshape(n_sec, capacity, width + LANES), 'user',...  23.3 us
    pallas_call x1, Pallas kernels, on_device(): pl.pallas_call(functools.partial(embed_kernel, window, sess), out_shape=(...  6.54 us
    ppermute x1, waiting for transfers between devices, on_device(): lax.ppermute(far, 'tm', [(t, t - window) for t in range(window, n_tm)])  5.01 us
  transfers between devices with their start and end apart: 1, of which 1 were waited for; matrix products, arithmetic and copies ran while one was open for 0% of the time, Pallas kernels for 0%

profile of v2, /device:TPU:1, one launch (start us, length us, event | category | flops | bytes accessed | tf_op | source)
XLA Modules:
  0.0 76.5 jit_solution(17597428970358944109)
XLA Ops:
  1.3 6.5 %embed.1 = (bf16[16,264,128]{2,1,0:T(8,128)(2,1)S(1)}, bf16[264,128]{1,0:T(8,128)(2,1)S(1)}) custom-call(s32[1,1]{1,0:T(1,128)S(6)} %copy.11.count_ref, bf16[1024,512]{1,0:T(8,128)(2,1)} %bitcast.10, bf16[512,1024]{1,0:T(8,128)(2,1)} %w1_ref.1, f32[1,1024]{1,0:T(1,128)} %bitcast.11, bf16[1024,512]{1,0:T(8,128)(2,1)} %w2_ref.1, s32[1,1024]{1,0:T(1,128)} %ids_ref.1), custom_call_target="tpu_custom_call" | custom-call | tf_op jit(solution)/shard_map/embed/pallas_call | solution.py:163
  7.8 36.9 %all_to_all.10.recv_ref = bf16[16,264,128]{2,1,0:T(8,128)(2,1)S(1)} all-to-all(bf16[16,264,128]{2,1,0:T(8,128)(2,1)S(1)} %get-tuple-element.6), channel_id=1, replica_groups={{0,16,32,48,64,80,96,112,128,144,160,176,192,208,224,240},{256,272,288,..., dimensions={0} | all-to-all | bytes 2162688 | tf_op jit(solution)/shard_map/all_to_all | solution.py:175
  44.7 0.2 far.1
  44.9 1.3 %collective-permute-start = (bf16[264,128]{1,0:T(8,128)(2,1)S(1)}, bf16[264,128]{1,0:T(8,128)(2,1)S(1)}, u32[]{:S(2)}, u32[]{:S(2)}) collective-permute-start(bf16[264,128]{1,0:T(8,128)(2,1)S(1)} %far.1), channel_id=1, source_target_pairs={{256,0},{272,16},{288,32},{304,48},{320,64},{336,80},{352,96},{368... | collective-permute-start | bytes 202760 | tf_op jit(solution)/shard_map/ppermute | solution.py:183
  46.2 0.2 near.1.near_ref
  46.5 5.0 %collective-permute-done.got_ref = bf16[264,128]{1,0:T(8,128)(2,1)S(1)} collective-permute-done((bf16[264,128]{1,0:T(8,128)(2,1)S(1)}, bf16[264,128]{1,0:T(8,128)(2,1)S(1)}, u32[]{:S(2)}, u32[]{:S(2)}) %collective-permute-start) | collective-permute-done | bytes 67616 | tf_op jit(solution)/shard_map/ppermute | solution.py:183
  51.5 1.1 %pack.1 = bf16[128,640]{1,0:T(8,128)(2,1)S(1)} custom-call(f32[264,128]{1,0:T(8,128)S(1)} %near.1.near_ref, bf16[264,128]{1,0:T(8,128)(2,1)S(1)} %collective-permute-done.got_ref, f32[1,512]{1,0:T(1,128)} %bitcast.12, f32[1,512]{1,0:T(1,128)} %bitcast.13, s32[1,64]{1,0:T(1,128)} %users_ref.1), custom_call_target="tpu_custom_call" | custom-call | tf_op jit(solution)/shard_map/pack/pallas_call | solution.py:191
  52.6 23.3 %all_to_all.11 = bf16[16,8,640]{2,1,0:T(8,128)(2,1)S(1)} all-to-all(bf16[16,8,640]{2,1,0:T(8,128)(2,1)S(1)} %bitcast.9), channel_id=1, replica_groups=mesh['tm'=32,'user'=16] {'user'}, dimensions={0} | all-to-all | bytes 327680 | tf_op jit(solution)/shard_map/all_to_all | solution.py:198
  75.8 0.7 unpack.1
Async XLA Ops:
  44.9 6.5 %collective-permute-start = (bf16[264,128]{1,0:T(8,128)(2,1)S(1)}, bf16[264,128]{1,0:T(8,128)(2,1)S(1)}, u32[]{:S(2)}, u32[]{:S(2)}) collective-permute-start(bf16[264,128]{1,0:T(8,128)(2,1)S(1)} %far.1), channel_id=1, source_target_pairs={{256,0},{272,16},{288,32},{304,48},{320,64},{336,80},{352,96},{368... | collective-permute-start | bytes 202760 | tf_op jit(solution)/shard_map/ppermute | solution.py:183

commit v3 on v2

v3 whole, which is shorter than its diff:
```python
import functools

import jax
import jax.numpy as jnp
from jax import lax
from jax.experimental import pallas as pl
from jax.experimental.pallas import tpu as pltpu
from jax.sharding import PartitionSpec as P

LANES = 128
DIGIT = 256.0


def count_tile(row):
    high = jnp.floor(row * (1.0 / DIGIT))
    low = row - high * DIGIT
    at = lax.broadcasted_iota(jnp.int32, (8, LANES), 0)
    return jnp.where(at == 0, high, jnp.where(at == 1, low, 0.0))


def gelu(x):
    half = 0.5 * x
    inner = x * (0.7978845608028654 + 0.035677408136300125 * (x * x))
    return half + half * jnp.tanh(inner)


def embed_kernel(window, sess, step, count_ref, ev_ref, w1_ref, b1_ref, w2_ref, ids_ref, out_ref, far_ref, vec, acc, counted):
    rows, width = ev_ref.shape
    groups = width // LANES
    pick = window * sess
    t = lax.axis_index("tm")
    for c in range(rows // step):
        at = pl.ds(c * step, step)
        h = jnp.dot(ev_ref[at, :], w1_ref[...], preferred_element_type=jnp.float32)
        h = gelu(h + b1_ref[...]).astype(jnp.bfloat16)
        vec[at, :] = jnp.dot(h, w2_ref[...], preferred_element_type=jnp.float32).astype(jnp.bfloat16)
    ids = ids_ref[...]
    far = (ids // sess) == t - window
    target = jnp.where(far, pick + ids % sess, ids % pick)
    valid = lax.broadcasted_iota(jnp.int32, ids.shape, 1) < count_ref[0, 0]
    target = jnp.where(valid, target, -1)
    total = pick + sess
    onehot = jnp.where(lax.broadcasted_iota(jnp.int32, (total, rows), 0) == target, 1.0, 0.0)
    counted[...] = jnp.broadcast_to(jnp.sum(onehot, axis=1, keepdims=True), counted.shape)
    acc[...] = jnp.dot(onehot.astype(jnp.bfloat16), vec[...], preferred_element_type=jnp.float32)
    per = LANES // sess
    row = lax.broadcasted_iota(jnp.int32, (LANES, LANES), 0)
    lane = lax.broadcasted_iota(jnp.int32, (LANES, LANES), 1)
    for c in range(pick // LANES):
        found = jnp.where(row == lane, counted[c * LANES : (c + 1) * LANES, :], 0.0)
        tile = count_tile(jnp.sum(found, axis=0, keepdims=True)).astype(jnp.bfloat16)
        for r in range(c * per, (c + 1) * per):
            for g in range(groups):
                out_ref[r, g * sess : (g + 1) * sess, :] = acc[
                    r * sess : (r + 1) * sess, g * LANES : (g + 1) * LANES
                ].astype(jnp.bfloat16)
            out_ref[r, groups * sess :, :] = tile
    for g in range(groups):
        far_ref[g * sess : (g + 1) * sess, :] = acc[pick:, g * LANES : (g + 1) * LANES].astype(jnp.bfloat16)
    spot = row[:sess] + sess * lax.rem(t, per)
    found = jnp.where(spot == lane[:sess], counted[pick:, :], 0.0)
    far_ref[groups * sess :, :] = count_tile(jnp.sum(found, axis=0, keepdims=True)).astype(jnp.bfloat16)


def far_kernel(window, recv_ref, far_ref, out_ref):
    me = lax.rem(lax.axis_index("tm"), window)
    total = far_ref[...].astype(jnp.float32)
    for j in range(window - 1):
        total += jnp.where(j < me, recv_ref[j].astype(jnp.float32), 0.0)
    data = total.shape[0] - 8
    out_ref[:data, :] = total[:data].astype(jnp.bfloat16)
    out_ref[data:, :] = count_tile(DIGIT * total[data : data + 1] + total[data + 1 : data + 2]).astype(jnp.bfloat16)


def near_kernel(window, n_sec, recv_ref, users_ref, embed_ref, gain_ref, out_ref, assign_ref, named_ref, embed_out, gain_out):
    embed_out[...] = embed_ref[...]
    gain_out[...] = gain_ref[...]
    me = lax.rem(lax.axis_index("tm"), window)
    total = recv_ref[window - 1].astype(jnp.float32)
    for j in range(window - 1):
        total += jnp.where(j >= me, recv_ref[j].astype(jnp.float32), 0.0)
    out_ref[...] = total
    slots, sess = assign_ref.shape
    users = users_ref[...]
    section = lax.rem(users, n_sec)
    i0 = lax.broadcasted_iota(jnp.int32, (sess, sess), 0)
    i1 = lax.broadcasted_iota(jnp.int32, (sess, sess), 1)
    section_column = jnp.sum(jnp.where(i0 == i1, section, 0), axis=1, keepdims=True)
    rank = jnp.sum(jnp.where((section_column == section) & (i0 < i1), 1, 0), axis=0, keepdims=True)
    slot = section * (slots // n_sec) + rank
    assign = lax.broadcasted_iota(jnp.int32, (slots, sess), 0) == slot
    assign_ref[...] = jnp.where(assign, 1.0, 0.0).astype(jnp.bfloat16)
    named = jnp.sum(jnp.where(assign, (users + 1).astype(jnp.float32), 0.0), axis=1, keepdims=True)
    high = jnp.floor(named * (1.0 / DIGIT))
    low = named - high * DIGIT
    lane = lax.broadcasted_iota(jnp.int32, (slots, LANES), 1)
    named_ref[...] = jnp.where(lane == 0, high, jnp.where(lane == 1, low, 0.0)).astype(jnp.bfloat16)


def pack_kernel(near_ref, got_ref, embed_ref, gain_ref, assign_ref, named_ref, out_ref):
    sess = assign_ref.shape[1]
    width = embed_ref.shape[1]
    groups = width // LANES
    t = lax.axis_index("tm")
    total = near_ref[...] + got_ref[...].astype(jnp.float32)
    data = groups * sess
    counts = DIGIT * total[data : data + 1] + total[data + 1 : data + 2]
    spot = lax.broadcasted_iota(jnp.int32, (sess, LANES), 0) + sess * lax.rem(t, LANES // sess)
    mine = spot == lax.broadcasted_iota(jnp.int32, (sess, LANES), 1)
    counts = jnp.sum(jnp.where(mine, counts, 0.0), axis=1, keepdims=True)
    least = jnp.maximum(counts, 1.0)
    weight = jnp.log1p(counts)
    mixed = [
        total[g * sess : (g + 1) * sess] / least + weight * embed_ref[:, g * LANES : (g + 1) * LANES]
        for g in range(groups)
    ]
    square = sum(m * m for m in mixed)
    scale = lax.rsqrt(jnp.sum(square, axis=1, keepdims=True) / width + 1e-06)
    for g, m in enumerate(mixed):
        at = slice(g * LANES, (g + 1) * LANES)
        row = (m * scale * gain_ref[:, at]).astype(jnp.bfloat16)
        out_ref[:, at] = jnp.dot(assign_ref[...], row, preferred_element_type=jnp.float32).astype(jnp.bfloat16)
    out_ref[:, width:] = named_ref[...]


def unpack_kernel(got_ref, rows_ref, users_ref):
    slots = got_ref.shape[0]
    width = rows_ref.shape[1]
    rows_ref[...] = got_ref[:, :width]
    digits = got_ref[:, width:].astype(jnp.float32)
    lane = lax.broadcasted_iota(jnp.int32, digits.shape, 1)
    column = jnp.sum(jnp.where(lane == 0, DIGIT * digits, jnp.where(lane == 1, digits, 0.0)), axis=1, keepdims=True)
    eye = lax.broadcasted_iota(jnp.int32, (slots, slots), 0) == lax.broadcasted_iota(jnp.int32, (slots, slots), 1)
    users_ref[...] = jnp.sum(jnp.where(eye, column, 0.0), axis=0, keepdims=True).astype(jnp.int32) - 1


def on_device(
    events,
    w_first,
    b_first,
    w_second,
    count_embed,
    norm_gain,
    event_session,
    event_count,
    session_user,
):
    rows, width = events.shape[1:]
    sess = session_user.shape[1]
    n_tm = lax.axis_size("tm")
    n_sec = lax.axis_size("user")
    capacity = max(2, 2 * sess // n_sec)
    window = n_tm // 2
    block = width // LANES * sess + 8
    bf16, f32 = jnp.bfloat16, jnp.float32
    vmem = pl.BlockSpec(memory_space=pltpu.VMEM)
    shape = jax.ShapeDtypeStruct
    kept = pltpu.VMEM
    pin = functools.partial(pltpu.with_memory_space_constraint, memory_space=pltpu.VMEM)
    blocks, far = pl.pallas_call(
        functools.partial(embed_kernel, window, sess, 1024),
        out_shape=(kept((window, block, LANES), bf16), kept((block, LANES), bf16)),
        in_specs=[pl.BlockSpec(memory_space=pltpu.SMEM)] + [vmem] * 5,
        out_specs=(vmem, vmem),
        scratch_shapes=[
            pltpu.VMEM((rows, width), bf16),
            pltpu.VMEM(((window + 1) * sess, width), f32),
            pltpu.VMEM(((window + 1) * sess, LANES), f32),
        ],
        name="embed",
    )(event_count, events[0], w_first, b_first[None], w_second, event_session)
    groups = [[first + j for j in range(window)] for first in range(0, n_tm, window)]
    arrived = lax.all_to_all(blocks, "tm", 0, 0, tiled=True, axis_index_groups=groups)
    far = pl.pallas_call(
        functools.partial(far_kernel, window),
        out_shape=kept((block, LANES), bf16),
        in_specs=[vmem, vmem],
        out_specs=vmem,
        name="far",
    )(pin(arrived), pin(far))
    got = lax.ppermute(far, "tm", [(t, t - window) for t in range(window, n_tm)])
    slots = n_sec * capacity
    near, assign, named, embed, gain = pl.pallas_call(
        functools.partial(near_kernel, window, n_sec),
        out_shape=(
            kept((block, LANES), f32),
            kept((slots, sess), bf16),
            kept((slots, LANES), bf16),
            kept((1, width), f32),
            kept((1, width), f32),
        ),
        in_specs=[vmem] * 4,
        out_specs=[vmem] * 5,
        name="near",
    )(pin(arrived), session_user, count_embed[None], norm_gain[None])
    outgoing = pl.pallas_call(
        pack_kernel,
        out_shape=kept((slots, width + LANES), bf16),
        in_specs=[vmem] * 6,
        out_specs=vmem,
        name="pack",
    )(*map(pin, (near, got, embed, gain, assign, named)))
    routed = lax.all_to_all(
        outgoing.reshape(n_sec, capacity, width + LANES), "user", 0, 0, tiled=True
    ).reshape(n_sec * capacity, width + LANES)
    section_rows, section_users = pl.pallas_call(
        unpack_kernel,
        out_shape=(shape((n_sec * capacity, width), bf16), shape((1, n_sec * capacity), jnp.int32)),
        in_specs=[vmem],
        out_specs=(vmem, vmem),
        name="unpack",
    )(pin(routed))
    return (section_rows[None, None], section_users[None])


def solution(mesh):
    in_specs = (
        P("user", "tm", None),
        P(),
        P(),
        P(),
        P(),
        P(),
        P("user", "tm"),
        P("user", "tm"),
        P("user", "tm"),
    )
    out_specs = (P("tm", "user", None, None), P("tm", "user", None))
    return jax.shard_map(
        on_device, mesh=mesh, in_specs=in_specs, out_specs=out_specs, check_vma=False
    )
```

time: 76.8 us -> 75.4 us (0.982)
  waiting for transfers between devices: 5.01 us -> 4.07 us
    ppermute x1, waiting for transfers between devices: 5.01 us -> 4.07 us  [on_device(): lax.ppermute(far, 'tm', [(t, t - window) for t in range(window, n_tm)])]
  transfers between devices with their start and end apart: 1 -> 1, of which waited for: 1 -> 1; matrix products, arithmetic and copies ran while one was open for 0% -> 0% of each run, Pallas kernels for 0% -> 2%
where the time goes in v3:
time: 75.4 us; the launch traced here: 75.1 us
  blocking collectives  60.2 us (80%)
  Pallas kernels  8.29 us (11%)
  waiting for transfers between devices  4.07 us (5%)
  between operations  1.31 us (2%)
  starting transfers between devices  1.29 us (2%)
    all_to_all x1, blocking collectives, on_device(): lax.all_to_all(blocks, 'tm', 0, 0, tiled=True, axis_index_groups=groups)  36.9 us
    all_to_all x1, blocking collectives, on_device(): lax.all_to_all(outgoing.reshape(n_sec, capacity, width + LANES), 'user',...  23.3 us
    pallas_call x1, Pallas kernels, on_device(): pl.pallas_call(functools.partial(embed_kernel, window, sess, 1024), out_s...  5.87 us
    ppermute x1, waiting for transfers between devices, on_device(): lax.ppermute(far, 'tm', [(t, t - window) for t in range(window, n_tm)])  4.07 us
  transfers between devices with their start and end apart: 1, of which 1 were waited for; matrix products, arithmetic and copies ran while one was open for 0% of the time, Pallas kernels for 2%

profile of v3, /device:TPU:1, one launch (start us, length us, event | category | flops | bytes accessed | tf_op | source)
XLA Modules:
  0.0 75.1 jit_solution(17477495447324841221)
XLA Ops:
  1.3 5.9 %embed.1 = (bf16[16,264,128]{2,1,0:T(8,128)(2,1)S(1)}, bf16[264,128]{1,0:T(8,128)(2,1)S(1)}) custom-call(s32[1,1]{1,0:T(1,128)S(6)} %copy.11.count_ref, bf16[1024,512]{1,0:T(8,128)(2,1)} %bitcast.10, bf16[512,1024]{1,0:T(8,128)(2,1)} %w1_ref.1, f32[1,1024]{1,0:T(1,128)} %bitcast.11, bf16[1024,512]{1,0:T(8,128)(2,1)} %w2_ref.1, s32[1,1024]{1,0:T(1,128)} %ids_ref.1), custom_call_target="tpu_custom_call" | custom-call | tf_op jit(solution)/shard_map/embed/pallas_call | solution.py:160
  7.2 36.9 %all_to_all.10.recv_ref = bf16[16,264,128]{2,1,0:T(8,128)(2,1)S(1)} all-to-all(bf16[16,264,128]{2,1,0:T(8,128)(2,1)S(1)} %get-tuple-element.11), channel_id=1, replica_groups={{0,16,32,48,64,80,96,112,128,144,160,176,192,208,224,240},{256,272,288,..., dimensions={0} | all-to-all | bytes 2162688 | tf_op jit(solution)/shard_map/all_to_all | solution.py:173
  44.1 0.2 far.1
  44.3 1.3 %collective-permute-start = (bf16[264,128]{1,0:T(8,128)(2,1)S(1)}, bf16[264,128]{1,0:T(8,128)(2,1)S(1)}, u32[]{:S(2)}, u32[]{:S(2)}) collective-permute-start(bf16[264,128]{1,0:T(8,128)(2,1)S(1)} %far.1), channel_id=1, source_target_pairs={{256,0},{272,16},{288,32},{304,48},{320,64},{336,80},{352,96},{368... | collective-permute-start | bytes 202760 | tf_op jit(solution)/shard_map/ppermute | solution.py:181
  45.6 1.2 %near.1 = (f32[264,128]{1,0:T(8,128)S(1)}, bf16[128,64]{1,0:T(8,128)(2,1)S(1)}, bf16[128,128]{1,0:T(8,128)(2,1)S(1)}, f32[1,512]{1,0:T(1,128)S(1)}, f32[1,512]{1,0:T(1,128)S(1)}) custom-call(bf16[16,264,128]{2,1,0:T(8,128)(2,1)S(1)} %all_to_all.10.recv_ref, s32[1,64]{1,0:T(1,128)} %users_ref.1, f32[1,512]{1,0:T(1,128)} %bitcast.12, f32[1,512]{1,0:T(1,128)} %bitcast.13), custom_call_target="tpu_custom_call" | custom-call | tf_op jit(solution)/shard_map/near/pallas_call | solution.py:183
  46.8 4.1 %collective-permute-done.got_ref = bf16[264,128]{1,0:T(8,128)(2,1)S(1)} collective-permute-done((bf16[264,128]{1,0:T(8,128)(2,1)S(1)}, bf16[264,128]{1,0:T(8,128)(2,1)S(1)}, u32[]{:S(2)}, u32[]{:S(2)}) %collective-permute-start) | collective-permute-done | bytes 67616 | tf_op jit(solution)/shard_map/ppermute | solution.py:181
  50.8 0.4 pack.1
  51.2 23.3 %all_to_all.11 = bf16[16,8,640]{2,1,0:T(8,128)(2,1)S(1)} all-to-all(bf16[16,8,640]{2,1,0:T(8,128)(2,1)S(1)} %bitcast.8), channel_id=1, replica_groups=mesh['tm'=32,'user'=16] {'user'}, dimensions={0} | all-to-all | bytes 327680 | tf_op jit(solution)/shard_map/all_to_all | solution.py:203
  74.5 0.7 unpack.1
Async XLA Ops:
  44.3 6.5 %collective-permute-start = (bf16[264,128]{1,0:T(8,128)(2,1)S(1)}, bf16[264,128]{1,0:T(8,128)(2,1)S(1)}, u32[]{:S(2)}, u32[]{:S(2)}) collective-permute-start(bf16[264,128]{1,0:T(8,128)(2,1)S(1)} %far.1), channel_id=1, source_target_pairs={{256,0},{272,16},{288,32},{304,48},{320,64},{336,80},{352,96},{368... | collective-permute-start | bytes 202760 | tf_op jit(solution)/shard_map/ppermute | solution.py:181

commit v4 on v3

--- a/solution.py
+++ b/solution.py
@@ -24,16 +24,17 @@
     return half + half * jnp.tanh(inner)
 
 
-def embed_kernel(window, sess, step, count_ref, ev_ref, w1_ref, b1_ref, w2_ref, ids_ref, out_ref, far_ref, vec, acc, counted):
-    rows, width = ev_ref.shape
+def hidden_kernel(ev_ref, w1_ref, b1_ref, out_ref):
+    h = jnp.dot(ev_ref[...], w1_ref[...], preferred_element_type=jnp.float32)
+    out_ref[...] = gelu(h + b1_ref[...]).astype(jnp.bfloat16)
+
+
+def sums_kernel(window, sess, count_ref, hidden_ref, w2_ref, ids_ref, out_ref, far_ref, acc, counted):
+    rows, width = hidden_ref.shape[0], w2_ref.shape[1]
     groups = width // LANES
     pick = window * sess
     t = lax.axis_index("tm")
-    for c in range(rows // step):
-        at = pl.ds(c * step, step)
-        h = jnp.dot(ev_ref[at, :], w1_ref[...], preferred_element_type=jnp.float32)
-        h = gelu(h + b1_ref[...]).astype(jnp.bfloat16)
-        vec[at, :] = jnp.dot(h, w2_ref[...], preferred_element_type=jnp.float32).astype(jnp.bfloat16)
+    vec = jnp.dot(hidden_ref[...], w2_ref[...], preferred_element_type=jnp.float32).astype(jnp.bfloat16)
     ids = ids_ref[...]
     far = (ids // sess) == t - window
     target = jnp.where(far, pick + ids % sess, ids % pick)
@@ -42,7 +43,7 @@
     total = pick + sess
     onehot = jnp.where(lax.broadcasted_iota(jnp.int32, (total, rows), 0) == target, 1.0, 0.0)
     counted[...] = jnp.broadcast_to(jnp.sum(onehot, axis=1, keepdims=True), counted.shape)
-    acc[...] = jnp.dot(onehot.astype(jnp.bfloat16), vec[...], preferred_element_type=jnp.float32)
+    acc[...] = jnp.dot(onehot.astype(jnp.bfloat16), vec, preferred_element_type=jnp.float32)
     per = LANES // sess
     row = lax.broadcasted_iota(jnp.int32, (LANES, LANES), 0)
     lane = lax.broadcasted_iota(jnp.int32, (LANES, LANES), 1)
@@ -154,21 +155,35 @@
     block = width // LANES * sess + 8
     bf16, f32 = jnp.bfloat16, jnp.float32
     vmem = pl.BlockSpec(memory_space=pltpu.VMEM)
+    here = functools.partial(pltpu.with_memory_space_constraint, memory_space=pltpu.HBM)
     shape = jax.ShapeDtypeStruct
     kept = pltpu.VMEM
     pin = functools.partial(pltpu.with_memory_space_constraint, memory_space=pltpu.VMEM)
+    units = w_first.shape[1]
+    grant = pltpu.CompilerParams(vmem_limit_bytes=24 * 1024 * 1024)
+    hidden = pl.pallas_call(
+        hidden_kernel,
+        out_shape=kept((rows, units), bf16),
+        in_specs=[vmem] * 3,
+        out_specs=vmem,
+        compiler_params=grant,
+        cost_estimate=pl.CostEstimate(
+            flops=2 * rows * width * units, transcendentals=rows * units, bytes_accessed=2 * width * (rows + units)
+        ),
+        name="hidden",
+    )(*map(here, (events[0], w_first, b_first[None])))
     blocks, far = pl.pallas_call(
-        functools.partial(embed_kernel, window, sess, 1024),
+        functools.partial(sums_kernel, window, sess),
         out_shape=(kept((window, block, LANES), bf16), kept((block, LANES), bf16)),
-        in_specs=[pl.BlockSpec(memory_space=pltpu.SMEM)] + [vmem] * 5,
+        in_specs=[pl.BlockSpec(memory_space=pltpu.SMEM)] + [vmem] * 3,
         out_specs=(vmem, vmem),
         scratch_shapes=[
-            pltpu.VMEM((rows, width), bf16),
             pltpu.VMEM(((window + 1) * sess, width), f32),
             pltpu.VMEM(((window + 1) * sess, LANES), f32),
         ],
-        name="embed",
-    )(event_count, events[0], w_first, b_first[None], w_second, event_session)
+        compiler_params=grant,
+        name="sums",
+    )(event_count, *map(pin, (hidden, w_second, event_session)))
     groups = [[first + j for j in range(window)] for first in range(0, n_tm, window)]
     arrived = lax.all_to_all(blocks, "tm", 0, 0, tiled=True, axis_index_groups=groups)
     far = pl.pallas_call(

time: 75.4 us -> 75.7 us (level)
    pallas_call x1 -> x2, Pallas kernels: 5.87 us -> 6.14 us  [the longest x1 3.57 us: on_device(): pl.pallas_call(hidden_kernel, out_shape=kept((rows, units), bf16), in_spe...]
where the time goes in v4:
time: 75.7 us; the launch traced here: 75.5 us
  blocking collectives  60.2 us (80%)
  Pallas kernels  8.56 us (11%)
  waiting for transfers between devices  4.07 us (5%)
  between operations  1.35 us (2%)
  starting transfers between devices  1.29 us (2%)
    all_to_all x1, blocking collectives, on_device(): lax.all_to_all(blocks, 'tm', 0, 0, tiled=True, axis_index_groups=groups)  36.9 us
    all_to_all x1, blocking collectives, on_device(): lax.all_to_all(outgoing.reshape(n_sec, capacity, width + LANES), 'user',...  23.3 us
    ppermute x1, waiting for transfers between devices, on_device(): lax.ppermute(far, 'tm', [(t, t - window) for t in range(window, n_tm)])  4.07 us
    pallas_call x1, Pallas kernels, on_device(): pl.pallas_call(hidden_kernel, out_shape=kept((rows, units), bf16), in_spe...  3.57 us
    pallas_call x1, Pallas kernels, on_device(): pl.pallas_call(functools.partial(sums_kernel, window, sess), out_shape=(k...  2.57 us
  transfers between devices with their start and end apart: 1, of which 1 were waited for; matrix products, arithmetic and copies ran while one was open for 0% of the time, Pallas kernels for 2%

profile of v4, /device:TPU:1, one launch (start us, length us, event | category | flops | bytes accessed | tf_op | source)
XLA Modules:
  0.0 75.5 jit_solution(12421964473063273854)
XLA Ops:
  1.3 0.0 copy-start
  1.3 0.0 copy-start.1
  1.3 3.6 %hidden.1.hidden_ref = bf16[1024,1024]{1,0:T(8,128)(2,1)S(1)} custom-call(bf16[1024,512]{1,0:T(8,128)(2,1)} %bitcast.10, bf16[512,1024]{1,0:T(8,128)(2,1)} %w1_ref.1, f32[1,1024]{1,0:T(1,128)} %bitcast.11), custom_call_target="tpu_custom_call" | custom-call | flops 1073741824 | bytes 2097152 | tf_op jit(solution)/shard_map/hidden/pallas_call | solution.py:164
  4.9 0.0 copy-done
  4.9 0.0 copy-done.1
  4.9 2.6 %sums.1 = (bf16[16,264,128]{2,1,0:T(8,128)(2,1)S(1)}, bf16[264,128]{1,0:T(8,128)(2,1)S(1)}) custom-call(s32[1,1]{1,0:T(1,128)S(6)} %copy.11.count_ref, bf16[1024,1024]{1,0:T(8,128)(2,1)S(1)} %hidden.1.hidden_ref, bf16[1024,512]{1,0:T(8,128)(2,1)S(1)} %copy-done, s32[1,1024]{1,0:T(1,128)S(1)} %copy-done.1), custom_call_target="tpu_custom_call" | custom-call | tf_op jit(solution)/shard_map/sums/pallas_call | solution.py:175
  7.5 36.9 %all_to_all.10.recv_ref = bf16[16,264,128]{2,1,0:T(8,128)(2,1)S(1)} all-to-all(bf16[16,264,128]{2,1,0:T(8,128)(2,1)S(1)} %get-tuple-element.11), channel_id=1, replica_groups={{0,16,32,48,64,80,96,112,128,144,160,176,192,208,224,240},{256,272,288,..., dimensions={0} | all-to-all | bytes 2162688 | tf_op jit(solution)/shard_map/all_to_all | solution.py:188
  44.4 0.2 far.1
  44.6 1.3 %collective-permute-start = (bf16[264,128]{1,0:T(8,128)(2,1)S(1)}, bf16[264,128]{1,0:T(8,128)(2,1)S(1)}, u32[]{:S(2)}, u32[]{:S(2)}) collective-permute-start(bf16[264,128]{1,0:T(8,128)(2,1)S(1)} %far.1), channel_id=1, source_target_pairs={{256,0},{272,16},{288,32},{304,48},{320,64},{336,80},{352,96},{368... | collective-permute-start | bytes 202760 | tf_op jit(solution)/shard_map/ppermute | solution.py:196
  45.9 1.2 %near.1 = (f32[264,128]{1,0:T(8,128)S(1)}, bf16[128,64]{1,0:T(8,128)(2,1)S(1)}, bf16[128,128]{1,0:T(8,128)(2,1)S(1)}, f32[1,512]{1,0:T(1,128)S(1)}, f32[1,512]{1,0:T(1,128)S(1)}) custom-call(bf16[16,264,128]{2,1,0:T(8,128)(2,1)S(1)} %all_to_all.10.recv_ref, s32[1,64]{1,0:T(1,128)} %users_ref.1, f32[1,512]{1,0:T(1,128)} %bitcast.12, f32[1,512]{1,0:T(1,128)} %bitcast.13), custom_call_target="tpu_custom_call" | custom-call | tf_op jit(solution)/shard_map/near/pallas_call | solution.py:198
  47.1 4.1 %collective-permute-done.got_ref = bf16[264,128]{1,0:T(8,128)(2,1)S(1)} collective-permute-done((bf16[264,128]{1,0:T(8,128)(2,1)S(1)}, bf16[264,128]{1,0:T(8,128)(2,1)S(1)}, u32[]{:S(2)}, u32[]{:S(2)}) %collective-permute-start) | collective-permute-done | bytes 67616 | tf_op jit(solution)/shard_map/ppermute | solution.py:196
  51.1 0.4 pack.1
  51.5 23.3 %all_to_all.11 = bf16[16,8,640]{2,1,0:T(8,128)(2,1)S(1)} all-to-all(bf16[16,8,640]{2,1,0:T(8,128)(2,1)S(1)} %bitcast.8), channel_id=1, replica_groups=mesh['tm'=32,'user'=16] {'user'}, dimensions={0} | all-to-all | bytes 327680 | tf_op jit(solution)/shard_map/all_to_all | solution.py:218
  74.8 0.7 unpack.1
Async XLA Ops:
  1.3 3.6 %copy-start = (bf16[1024,512]{1,0:T(8,128)(2,1)S(1)}, bf16[1024,512]{1,0:T(8,128)(2,1)}, u32[]{:S(2)}) copy-start(bf16[1024,512]{1,0:T(8,128)(2,1)} %w2_ref.1) | copy-start | bytes 3145732
  1.3 3.6 %copy-start.1 = (s32[1,1024]{1,0:T(1,128)S(1)}, s32[1,1024]{1,0:T(1,128)}, u32[]{:S(2)}) copy-start(s32[1,1024]{1,0:T(1,128)} %ids_ref.1) | copy-start | bytes 12292
  44.6 6.5 %collective-permute-start = (bf16[264,128]{1,0:T(8,128)(2,1)S(1)}, bf16[264,128]{1,0:T(8,128)(2,1)S(1)}, u32[]{:S(2)}, u32[]{:S(2)}) collective-permute-start(bf16[264,128]{1,0:T(8,128)(2,1)S(1)} %far.1), channel_id=1, source_target_pairs={{256,0},{272,16},{288,32},{304,48},{320,64},{336,80},{352,96},{368... | collective-permute-start | bytes 202760 | tf_op jit(solution)/shard_map/ppermute | solution.py:196

commit v5 on v3

--- a/solution.py
+++ b/solution.py
@@ -24,16 +24,26 @@
     return half + half * jnp.tanh(inner)
 
 
-def embed_kernel(window, sess, step, count_ref, ev_ref, w1_ref, b1_ref, w2_ref, ids_ref, out_ref, far_ref, vec, acc, counted):
+def embed_kernel(window, sess, step, count_ref, ev_hbm, w1_hbm, b1_hbm, w2_hbm, ids_hbm, out_ref, far_ref, vec, acc, counted, ev_ref, w1_ref, b1_ref, w2_ref, ids_ref, hidden, sems):
+    half = ev_ref.shape[0] // 2
+    parts = [pl.ds(k * half, half) for k in range(2)]
+    pairs = [(w1_hbm, w1_ref), (b1_hbm, b1_ref), (ev_hbm.at[parts[0], :], ev_ref.at[parts[0], :])]
+    pairs += [(ev_hbm.at[parts[1], :], ev_ref.at[parts[1], :]), (w2_hbm, w2_ref), (ids_hbm, ids_ref)]
+    loads = [pltpu.make_async_copy(src, dst, sems.at[k]) for k, (src, dst) in enumerate(pairs)]
+    for load in loads:
+        load.start()
     rows, width = ev_ref.shape
     groups = width // LANES
     pick = window * sess
     t = lax.axis_index("tm")
-    for c in range(rows // step):
-        at = pl.ds(c * step, step)
-        h = jnp.dot(ev_ref[at, :], w1_ref[...], preferred_element_type=jnp.float32)
-        h = gelu(h + b1_ref[...]).astype(jnp.bfloat16)
-        vec[at, :] = jnp.dot(h, w2_ref[...], preferred_element_type=jnp.float32).astype(jnp.bfloat16)
+    for part, waits in zip(parts, (loads[:3], loads[3:4])):
+        for load in waits:
+            load.wait()
+        h = jnp.dot(ev_ref[part, :], w1_ref[...], preferred_element_type=jnp.float32)
+        hidden[part, :] = gelu(h + b1_ref[...]).astype(jnp.bfloat16)
+    for load in loads[4:]:
+        load.wait()
+    vec[...] = jnp.dot(hidden[...], w2_ref[...], preferred_element_type=jnp.float32).astype(jnp.bfloat16)
     ids = ids_ref[...]
     far = (ids // sess) == t - window
     target = jnp.where(far, pick + ids % sess, ids % pick)
@@ -154,21 +164,30 @@
     block = width // LANES * sess + 8
     bf16, f32 = jnp.bfloat16, jnp.float32
     vmem = pl.BlockSpec(memory_space=pltpu.VMEM)
+    hbm = pl.BlockSpec(memory_space=pltpu.HBM)
+    here = functools.partial(pltpu.with_memory_space_constraint, memory_space=pltpu.HBM)
     shape = jax.ShapeDtypeStruct
     kept = pltpu.VMEM
     pin = functools.partial(pltpu.with_memory_space_constraint, memory_space=pltpu.VMEM)
     blocks, far = pl.pallas_call(
         functools.partial(embed_kernel, window, sess, 1024),
         out_shape=(kept((window, block, LANES), bf16), kept((block, LANES), bf16)),
-        in_specs=[pl.BlockSpec(memory_space=pltpu.SMEM)] + [vmem] * 5,
+        in_specs=[pl.BlockSpec(memory_space=pltpu.SMEM)] + [hbm] * 5,
         out_specs=(vmem, vmem),
         scratch_shapes=[
             pltpu.VMEM((rows, width), bf16),
             pltpu.VMEM(((window + 1) * sess, width), f32),
             pltpu.VMEM(((window + 1) * sess, LANES), f32),
+            pltpu.VMEM((rows, width), bf16),
+            pltpu.VMEM(w_first.shape, bf16),
+            pltpu.VMEM((1, w_first.shape[1]), f32),
+            pltpu.VMEM(w_second.shape, bf16),
+            pltpu.VMEM((1, rows), jnp.int32),
+            pltpu.VMEM((rows, w_first.shape[1]), bf16),
+            pltpu.SemaphoreType.DMA((6,)),
         ],
         name="embed",
-    )(event_count, events[0], w_first, b_first[None], w_second, event_session)
+    )(event_count, *map(here, (events[0], w_first, b_first[None], w_second, event_session)))
     groups = [[first + j for j in range(window)] for first in range(0, n_tm, window)]
     arrived = lax.all_to_all(blocks, "tm", 0, 0, tiled=True, axis_index_groups=groups)
     far = pl.pallas_call(

time: 75.4 us -> 75.6 us (level)
  no operation moved by 1% of the time
where the time goes in v5:
time: 75.6 us; the launch traced here: 75.4 us
  blocking collectives  60.2 us (80%)
  Pallas kernels  8.56 us (11%)
  waiting for transfers between devices  4.07 us (5%)
  between operations  1.31 us (2%)
  starting transfers between devices  1.29 us (2%)
    all_to_all x1, blocking collectives, on_device(): lax.all_to_all(blocks, 'tm', 0, 0, tiled=True, axis_index_groups=groups)  36.9 us
    all_to_all x1, blocking collectives, on_device(): lax.all_to_all(outgoing.reshape(n_sec, capacity, width + LANES), 'user',...  23.3 us
    pallas_call x1, Pallas kernels, on_device(): pl.pallas_call(functools.partial(embed_kernel, window, sess, 1024), out_s...  6.14 us
    ppermute x1, waiting for transfers between devices, on_device(): lax.ppermute(far, 'tm', [(t, t - window) for t in range(window, n_tm)])  4.07 us
  transfers between devices with their start and end apart: 1, of which 1 were waited for; matrix products, arithmetic and copies ran while one was open for 0% of the time, Pallas kernels for 2%

profile of v5, /device:TPU:1, one launch (start us, length us, event | category | flops | bytes accessed | tf_op | source)
XLA Modules:
  0.0 75.4 jit_solution(7911841238891647106)
XLA Ops:
  1.3 6.1 %embed.1 = (bf16[16,264,128]{2,1,0:T(8,128)(2,1)S(1)}, bf16[264,128]{1,0:T(8,128)(2,1)S(1)}) custom-call(s32[1,1]{1,0:T(1,128)S(6)} %copy.11.count_ref, bf16[1024,512]{1,0:T(8,128)(2,1)} %bitcast.10, bf16[512,1024]{1,0:T(8,128)(2,1)} %w1_hbm.1, f32[1,1024]{1,0:T(1,128)} %bitcast.11, bf16[1024,512]{1,0:T(8,128)(2,1)} %w2_hbm.1, s32[1,1024]{1,0:T(1,128)} %ids_hbm.1), custom_call_target="tpu_custom_call" | custom-call | tf_op jit(solution)/shard_map/embed/pallas_call | solution.py:172
  7.4 36.9 %all_to_all.10.recv_ref = bf16[16,264,128]{2,1,0:T(8,128)(2,1)S(1)} all-to-all(bf16[16,264,128]{2,1,0:T(8,128)(2,1)S(1)} %get-tuple-element.11), channel_id=1, replica_groups={{0,16,32,48,64,80,96,112,128,144,160,176,192,208,224,240},{256,272,288,..., dimensions={0} | all-to-all | bytes 2162688 | tf_op jit(solution)/shard_map/all_to_all | solution.py:192
  44.3 0.2 far.1
  44.5 1.3 %collective-permute-start = (bf16[264,128]{1,0:T(8,128)(2,1)S(1)}, bf16[264,128]{1,0:T(8,128)(2,1)S(1)}, u32[]{:S(2)}, u32[]{:S(2)}) collective-permute-start(bf16[264,128]{1,0:T(8,128)(2,1)S(1)} %far.1), channel_id=1, source_target_pairs={{256,0},{272,16},{288,32},{304,48},{320,64},{336,80},{352,96},{368... | collective-permute-start | bytes 202760 | tf_op jit(solution)/shard_map/ppermute | solution.py:200
  45.8 1.2 %near.1 = (f32[264,128]{1,0:T(8,128)S(1)}, bf16[128,64]{1,0:T(8,128)(2,1)S(1)}, bf16[128,128]{1,0:T(8,128)(2,1)S(1)}, f32[1,512]{1,0:T(1,128)S(1)}, f32[1,512]{1,0:T(1,128)S(1)}) custom-call(bf16[16,264,128]{2,1,0:T(8,128)(2,1)S(1)} %all_to_all.10.recv_ref, s32[1,64]{1,0:T(1,128)} %users_ref.1, f32[1,512]{1,0:T(1,128)} %bitcast.12, f32[1,512]{1,0:T(1,128)} %bitcast.13), custom_call_target="tpu_custom_call" | custom-call | tf_op jit(solution)/shard_map/near/pallas_call | solution.py:202
  47.0 4.1 %collective-permute-done.got_ref = bf16[264,128]{1,0:T(8,128)(2,1)S(1)} collective-permute-done((bf16[264,128]{1,0:T(8,128)(2,1)S(1)}, bf16[264,128]{1,0:T(8,128)(2,1)S(1)}, u32[]{:S(2)}, u32[]{:S(2)}) %collective-permute-start) | collective-permute-done | bytes 67616 | tf_op jit(solution)/shard_map/ppermute | solution.py:200
  51.1 0.4 pack.1
  51.5 23.3 %all_to_all.11 = bf16[16,8,640]{2,1,0:T(8,128)(2,1)S(1)} all-to-all(bf16[16,8,640]{2,1,0:T(8,128)(2,1)S(1)} %bitcast.8), channel_id=1, replica_groups=mesh['tm'=32,'user'=16] {'user'}, dimensions={0} | all-to-all | bytes 327680 | tf_op jit(solution)/shard_map/all_to_all | solution.py:222
  74.7 0.7 unpack.1
Async XLA Ops:
  44.5 6.5 %collective-permute-start = (bf16[264,128]{1,0:T(8,128)(2,1)S(1)}, bf16[264,128]{1,0:T(8,128)(2,1)S(1)}, u32[]{:S(2)}, u32[]{:S(2)}) collective-permute-start(bf16[264,128]{1,0:T(8,128)(2,1)S(1)} %far.1), channel_id=1, source_target_pairs={{256,0},{272,16},{288,32},{304,48},{320,64},{336,80},{352,96},{368... | collective-permute-start | bytes 202760 | tf_op jit(solution)/shard_map/ppermute | solution.py:200
